TPU v7x, 32 devices: a whole 2x2x4 slice. The times are simulated.
32 devices in a mesh: expert: 8 (over z, x), tensor: 4 (over y, core).
Axes of the slice: x: 2, y: 2, z: 4, core: 2. Of those that a mesh axis runs over, the one named last changes fastest.
Arguments:
- hidden_in: bfloat16 [4096, 2048], P('expert'), may hold values from -6 to 6
- doc_ids: int32 [8, 512], P('expert'), may hold values from 0 to 2, never falling along the last dimension, each value on 1 to 384 neighbouring positions
- routes: int32 [4096, 8], P('expert'), may hold values from 0 to 15, all different within a row
- out_grad: bfloat16 [4096, 2048], P('expert'), may hold values from -6 to 6
- norm1_gain: float32 [2048], replicated, may hold values from 0.5 to 1.5
- q_weight: bfloat16 [2048, 2048], P(None, 'tensor'), may hold values from -0.125 to 0.125
- k_weight: bfloat16 [2048, 2048], P(None, 'tensor'), may hold values from -0.125 to 0.125
- v_weight: bfloat16 [2048, 2048], P(None, 'tensor'), may hold values from -0.125 to 0.125
- o_weight: bfloat16 [2048, 2048], P(None, 'tensor'), may hold values from -1.5 to 1.5
- q_gain: float32 [128], replicated, may hold values from 0.5 to 1.5
- k_gain: float32 [128], replicated, may hold values from 0.5 to 1.5
- norm2_gain: float32 [2048], replicated, may hold values from 0.5 to 1.5
- router_weight: bfloat16 [2048, 16], replicated, may hold values from -0.0625 to 0.0625
- gate_weight: bfloat16 [16, 2048, 1024], P('expert', None, 'tensor'), may hold values from -0.125 to 0.125
- up_weight: bfloat16 [16, 2048, 1024], P('expert', None, 'tensor'), may hold values from -0.125 to 0.125
- down_weight: bfloat16 [16, 1024, 2048], P('expert', 'tensor'), may hold values from -0.5 to 0.5
Outputs:
- output: bfloat16 [4096, 2048], P('expert')
- input_grad: float32 [4096, 2048], P('expert')
- norm1_gain_grad: float32 [2048], P('expert')
- q_weight_grad: float32 [2048, 2048], P('expert', 'tensor')
- k_weight_grad: float32 [2048, 2048], P('expert', 'tensor')
- v_weight_grad: float32 [2048, 2048], P('expert', 'tensor')
- o_weight_grad: float32 [2048, 2048], P('expert', 'tensor')
- q_gain_grad: float32 [128], P('expert')
- k_gain_grad: float32 [128], P('expert')
- norm2_gain_grad: float32 [2048], P('expert')
- router_weight_grad: float32 [2048, 16], P('expert')
- gate_weight_grad: float32 [16, 2048, 1024], P('expert', None, 'tensor')
- up_weight_grad: float32 [16, 2048, 1024], P('expert', None, 'tensor')
- down_weight_grad: float32 [16, 1024, 2048], P('expert', 'tensor')
Inputs may be any that keep to these rules, and one draw needn't show every extreme that they name: Each row of routes names 8 different experts. `doc_ids`: within a packed row ids never fall; a document has at most 384 tokens.
All inputs are finite; a program needn't handle non-finite values.
Results may differ from a plain program's by a relative error of at most 0.024.
Values may be sent and summed in bfloat16 or wider, within the bound.
No kernel may reach another device: no remote copies, remote signals or barrier semaphores. Data moves between devices by JAX's collectives and lax.ppermute only.
A program may use at most 320 MiB of HBM per device.

v0:
```python
import jax
import jax.numpy as jnp
from jax import lax
from jax.sharding import PartitionSpec as P

epsilon = 1e-06
rope_base = 10000.0
masked_score = -1e30


def rms_scale(values):
    return lax.rsqrt(jnp.mean(values * values, axis=-1, keepdims=True) + epsilon)


def rotary(positions, head_size):
    half_size = head_size // 2
    freqs = rope_base ** (-2.0 * jnp.arange(half_size, dtype=jnp.float32) / head_size)
    angles = jnp.arange(positions, dtype=jnp.float32)[:, None] * freqs[None, :]
    cosine = jnp.cos(angles)
    sine = jnp.sin(angles)
    return (jnp.concatenate([cosine, cosine], -1), jnp.concatenate([sine, sine], -1))


def prep_heads(raw, gain, factor, cosine, sine, heads):
    shaped = raw.reshape(raw.shape[0], heads, -1)
    normed = shaped * rms_scale(shaped) * gain
    half_size = normed.shape[-1] // 2
    turned = jnp.concatenate([-normed[..., half_size:], normed[..., :half_size]], -1)
    return (normed * cosine[:, None, :] + turned * sine[:, None, :]) * factor


def slot_tables(route_rows, all_experts, capacity):
    num_tokens, num_picks = route_rows.shape
    flat_routes = route_rows.reshape(-1)
    onehot = (flat_routes[:, None] == jnp.arange(all_experts, dtype=jnp.int32)[None, :]).astype(
        jnp.int32
    )
    before = jnp.cumsum(onehot, axis=0) - onehot
    placed = jnp.sum(before * onehot, axis=1)
    slot_ids = jnp.where(placed < capacity, flat_routes * capacity + placed, all_experts * capacity)
    pair_ids = jnp.arange(num_tokens * num_picks, dtype=jnp.int32)
    pair_of = (
        jnp.full((all_experts * capacity + 1,), num_tokens * num_picks, jnp.int32)
        .at[slot_ids]
        .set(pair_ids)
    )
    return (slot_ids.reshape(num_tokens, num_picks), pair_of[:-1])


def on_device(
    hidden_in,
    doc_ids,
    routes,
    out_grad,
    norm1_gain,
    q_weight,
    k_weight,
    v_weight,
    o_weight,
    q_gain,
    k_gain,
    norm2_gain,
    router_weight,
    gate_weight,
    up_weight,
    down_weight,
):
    num_tokens, model_width = hidden_in.shape
    num_picks = routes.shape[1]
    head_size = q_gain.shape[0]
    local_heads = q_weight.shape[1] // head_size
    local_experts = gate_weight.shape[0]
    ffn_local = gate_weight.shape[2]
    expert_ranks = lax.axis_size("expert")
    tensor_ranks = lax.axis_size("tensor")
    all_experts = local_experts * expert_ranks
    capacity = tensor_ranks * (
        (9 * num_tokens * num_picks + 8 * all_experts * tensor_ranks - 1)
        // (8 * all_experts * tensor_ranks)
    )
    doc_row = doc_ids[0]
    cosine, sine = rotary(num_tokens, head_size)
    zero_row = jnp.zeros((1, model_width), jnp.bfloat16)
    inputs = hidden_in.astype(jnp.float32)
    scale_one = rms_scale(inputs)
    unit_one = inputs * scale_one
    normed_one = (unit_one * norm1_gain).astype(jnp.bfloat16)
    q_raw = jnp.dot(normed_one, q_weight, preferred_element_type=jnp.float32)
    k_raw = jnp.dot(normed_one, k_weight, preferred_element_type=jnp.float32)
    v_raw = jnp.dot(normed_one, v_weight, preferred_element_type=jnp.float32)

    def shape_heads(q_in, k_in, q_scale, k_scale):
        return (
            prep_heads(q_in, q_scale, head_size ** (-0.5), cosine, sine, local_heads),
            prep_heads(k_in, k_scale, 1.0, cosine, sine, local_heads),
        )

    head_vals, head_back = jax.vjp(shape_heads, q_raw, k_raw, q_gain, k_gain)
    queries = head_vals[0].astype(jnp.bfloat16)
    keys = head_vals[1].astype(jnp.bfloat16)
    values = v_raw.astype(jnp.bfloat16).reshape(num_tokens, local_heads, head_size)

    def block_scores():
        scores = jnp.einsum("qhd,khd->hqk", queries, keys, preferred_element_type=jnp.float32)
        return (
            jnp.where((doc_row[:, None] == doc_row[None, :])[None], scores, masked_score),
            queries,
        )

    scores, query_blk = block_scores()
    peak = jnp.max(scores, -1, keepdims=True)
    log_total = peak + jnp.log(jnp.sum(jnp.exp(scores - peak), -1, keepdims=True))
    weights = jnp.exp(scores - log_total).astype(jnp.bfloat16)
    block_outs = jnp.einsum("hqk,khd->qhd", weights, values, preferred_element_type=jnp.float32)
    attn_out = block_outs.reshape(num_tokens, local_heads * head_size).astype(jnp.bfloat16)
    attn_part = lax.dot_general(
        attn_out, o_weight, (((1,), (1,)), ((), ())), preferred_element_type=jnp.float32
    )
    attn_full = lax.psum(attn_part, "tensor")
    after_attn = inputs + attn_full
    scale_two = rms_scale(after_attn)
    unit_two = after_attn * scale_two
    normed_two = (unit_two * norm2_gain).astype(jnp.bfloat16)
    logits = jnp.dot(normed_two, router_weight, preferred_element_type=jnp.float32)
    pick_mask = routes[:, :, None] == jnp.arange(all_experts, dtype=jnp.int32)[None, None, :]
    chosen = jnp.sum(jnp.where(pick_mask, logits[:, None, :], 0.0), -1)
    gates = jax.nn.softmax(chosen, -1)
    slot_ids, pair_of = slot_tables(routes, all_experts, capacity)
    owners = pair_of // num_picks
    padded_rows = jnp.concatenate([normed_two, zero_row], 0)
    send_buf = jnp.take(padded_rows, owners, axis=0).reshape(
        expert_ranks, local_experts, capacity, model_width
    )
    slot_rows = lax.all_to_all(send_buf, "expert", split_axis=0, concat_axis=0, tiled=True)
    gate_up = jnp.concatenate([gate_weight, up_weight], 2)
    joint_pre = jnp.einsum("secd,edf->secf", slot_rows, gate_up, preferred_element_type=jnp.float32)
    gate_pre = joint_pre[..., :ffn_local]
    up_pre = joint_pre[..., ffn_local:]
    silu_gate = jax.nn.silu(gate_pre)
    hidden = (silu_gate * up_pre).astype(jnp.bfloat16)
    partial_out = jnp.einsum(
        "secf,efd->secd", hidden, down_weight, preferred_element_type=jnp.float32
    ).astype(jnp.bfloat16)
    out_grads = out_grad.astype(jnp.float32)
    mixture = jnp.zeros((num_tokens, model_width), jnp.float32)
    gate_dots = []
    returned = lax.all_to_all(
        partial_out, "expert", split_axis=0, concat_axis=0, tiled=True
    ).reshape(all_experts * capacity, model_width)
    returned = jnp.concatenate([returned, zero_row], 0)
    for rank_k in range(num_picks):
        picked = jnp.take(returned, slot_ids[:, rank_k], axis=0)
        mixture = mixture + gates[:, rank_k, None] * picked
        gate_dots.append(jnp.sum(out_grads * picked, -1))
    moe_full = lax.psum(mixture.astype(jnp.bfloat16), "tensor").astype(jnp.float32)
    output = (after_attn + moe_full).astype(jnp.bfloat16)
    dgate_part = jnp.stack(gate_dots, -1)
    padded_gates = jnp.concatenate([gates.reshape(-1), jnp.zeros((1,), jnp.float32)], 0)
    padded_grads = jnp.concatenate([out_grads, jnp.zeros((1, model_width), jnp.float32)], 0)
    slot_gate = jnp.take(padded_gates, pair_of, axis=0)
    grad_buf = (slot_gate[:, None] * jnp.take(padded_grads, owners, axis=0)).astype(jnp.bfloat16)
    grads_in = lax.all_to_all(
        grad_buf.reshape(expert_ranks, local_experts, capacity, model_width),
        "expert",
        split_axis=0,
        concat_axis=0,
        tiled=True,
    )
    dhidden = jnp.einsum(
        "secd,efd->secf", grads_in, down_weight, preferred_element_type=jnp.float32
    )
    down_grad = jnp.einsum("secf,secd->efd", hidden, grads_in, preferred_element_type=jnp.float32)
    sig_gate = jax.nn.sigmoid(gate_pre)
    dgate_pre = dhidden * up_pre * (sig_gate * (1.0 + gate_pre * (1.0 - sig_gate)))
    dup_pre = dhidden * silu_gate
    djoint = jnp.concatenate([dgate_pre, dup_pre], -1).astype(jnp.bfloat16)
    joint_grad = jnp.einsum("secd,secf->edf", slot_rows, djoint, preferred_element_type=jnp.float32)
    gate_grad = joint_grad[..., :ffn_local]
    up_grad = joint_grad[..., ffn_local:]
    dslot_in = jnp.einsum(
        "secf,edf->secd", djoint, gate_up, preferred_element_type=jnp.float32
    ).astype(jnp.bfloat16)
    dnormed_part = jnp.zeros((num_tokens, model_width), jnp.float32)
    came_back = lax.all_to_all(dslot_in, "expert", split_axis=0, concat_axis=0, tiled=True).reshape(
        all_experts * capacity, model_width
    )
    came_back = jnp.concatenate([came_back, zero_row], 0)
    for rank_k in range(num_picks):
        dnormed_part = dnormed_part + jnp.take(came_back, slot_ids[:, rank_k], axis=0)
    dnormed_exp, dgate_all = lax.psum((dnormed_part, dgate_part), "tensor")
    dsel = gates * (dgate_all - jnp.sum(gates * dgate_all, -1, keepdims=True))
    dlogits = jnp.sum(jnp.where(pick_mask, dsel[:, :, None], 0.0), 1).astype(jnp.bfloat16)
    router_grad = lax.dot_general(
        normed_two, dlogits, (((0,), (0,)), ((), ())), preferred_element_type=jnp.float32
    )
    dnormed_two = dnormed_exp + lax.dot_general(
        dlogits, router_weight, (((1,), (1,)), ((), ())), preferred_element_type=jnp.float32
    )
    norm2_grad = jnp.sum(dnormed_two * unit_two, 0)
    weighted_two = dnormed_two * norm2_gain
    dafter = out_grads + scale_two * (
        weighted_two - unit_two * jnp.mean(weighted_two * unit_two, -1, keepdims=True)
    )
    dattn = dafter.astype(jnp.bfloat16)
    o_grad = lax.dot_general(
        dattn, attn_out, (((0,), (0,)), ((), ())), preferred_element_type=jnp.float32
    )
    dattn_out = (
        jnp.dot(dattn, o_weight, preferred_element_type=jnp.float32)
        .astype(jnp.bfloat16)
        .reshape(num_tokens, local_heads, head_size)
    )
    scores, query_blk = block_scores()
    probs = jnp.exp(scores - log_total)
    dprobs = jnp.einsum("qhd,khd->hqk", dattn_out, values, preferred_element_type=jnp.float32)
    dscores = (probs * (dprobs - jnp.sum(probs * dprobs, -1, keepdims=True))).astype(jnp.bfloat16)
    dquery_blocks = jnp.einsum("hqk,khd->qhd", dscores, keys, preferred_element_type=jnp.float32)
    dkey = jnp.einsum("hqk,qhd->khd", dscores, query_blk, preferred_element_type=jnp.float32)
    dvalue = jnp.einsum(
        "hqk,qhd->khd", probs.astype(jnp.bfloat16), dattn_out, preferred_element_type=jnp.float32
    )
    dq_raw, dk_raw, q_gain_part, k_gain_part = head_back((dquery_blocks, dkey))
    dq_low = dq_raw.astype(jnp.bfloat16)
    dk_low = dk_raw.astype(jnp.bfloat16)
    dv_low = dvalue.reshape(num_tokens, local_heads * head_size).astype(jnp.bfloat16)
    contract_rows = (((0,), (0,)), ((), ()))
    contract_cols = (((1,), (1,)), ((), ()))
    q_grad = lax.dot_general(normed_one, dq_low, contract_rows, preferred_element_type=jnp.float32)
    k_grad = lax.dot_general(normed_one, dk_low, contract_rows, preferred_element_type=jnp.float32)
    v_grad = lax.dot_general(normed_one, dv_low, contract_rows, preferred_element_type=jnp.float32)
    dnormed_one = lax.dot_general(
        dq_low, q_weight, contract_cols, preferred_element_type=jnp.float32
    )
    dnormed_one = dnormed_one + lax.dot_general(
        dk_low, k_weight, contract_cols, preferred_element_type=jnp.float32
    )
    dnormed_one = dnormed_one + lax.dot_general(
        dv_low, v_weight, contract_cols, preferred_element_type=jnp.float32
    )
    dnormed_full, q_gain_sum, k_gain_sum = (
        lax.psum(dnormed_one.astype(jnp.bfloat16), "tensor").astype(jnp.float32),
        lax.psum(q_gain_part.astype(jnp.bfloat16), "tensor").astype(jnp.float32),
        lax.psum(k_gain_part.astype(jnp.bfloat16), "tensor").astype(jnp.float32),
    )
    norm1_grad = jnp.sum(dnormed_full * unit_one, 0)
    weighted_one = dnormed_full * norm1_gain
    input_grad = dafter + scale_one * (
        weighted_one - unit_one * jnp.mean(weighted_one * unit_one, -1, keepdims=True)
    )
    reduced = (
        lax.psum_scatter(
            q_grad.astype(jnp.bfloat16), "expert", scatter_dimension=0, tiled=True
        ).astype(jnp.float32),
        lax.psum_scatter(
            k_grad.astype(jnp.bfloat16), "expert", scatter_dimension=0, tiled=True
        ).astype(jnp.float32),
        lax.psum_scatter(
            v_grad.astype(jnp.bfloat16), "expert", scatter_dimension=0, tiled=True
        ).astype(jnp.float32),
        lax.psum_scatter(
            o_grad.astype(jnp.bfloat16), "expert", scatter_dimension=0, tiled=True
        ).astype(jnp.float32),
        lax.psum_scatter(
            router_grad.astype(jnp.bfloat16), "expert", scatter_dimension=0, tiled=True
        ).astype(jnp.float32),
        lax.psum_scatter(
            norm1_grad.astype(jnp.bfloat16), "expert", scatter_dimension=0, tiled=True
        ).astype(jnp.float32),
        lax.psum_scatter(
            norm2_grad.astype(jnp.bfloat16), "expert", scatter_dimension=0, tiled=True
        ).astype(jnp.float32),
        lax.psum_scatter(
            q_gain_sum.astype(jnp.bfloat16), "expert", scatter_dimension=0, tiled=True
        ).astype(jnp.float32),
        lax.psum_scatter(
            k_gain_sum.astype(jnp.bfloat16), "expert", scatter_dimension=0, tiled=True
        ).astype(jnp.float32),
    )
    return (
        output,
        input_grad,
        reduced[5],
        reduced[0],
        reduced[1],
        reduced[2],
        reduced[3],
        reduced[7],
        reduced[8],
        reduced[6],
        reduced[4],
        gate_grad,
        up_grad,
        down_grad,
    )


def solution(mesh):
    return jax.shard_map(
        on_device,
        mesh=mesh,
        in_specs=(
            P("expert", None),
            P("expert", None),
            P("expert", None),
            P("expert", None),
            P(),
            P(None, "tensor"),
            P(None, "tensor"),
            P(None, "tensor"),
            P(None, "tensor"),
            P(),
            P(),
            P(),
            P(),
            P("expert", None, "tensor"),
            P("expert", None, "tensor"),
            P("expert", "tensor", None),
        ),
        out_specs=(
            P("expert", None),
            P("expert", None),
            P("expert"),
            P("expert", "tensor"),
            P("expert", "tensor"),
            P("expert", "tensor"),
            P("expert", "tensor"),
            P("expert"),
            P("expert"),
            P("expert"),
            P("expert", None),
            P("expert", None, "tensor"),
            P("expert", None, "tensor"),
            P("expert", "tensor", None),
        ),
        check_vma=False,
    )
```

profile of v0, /device:TPU:0, one launch (start us, length us, event | category | flops | bytes accessed | tf_op | source)
XLA Modules:
  0.0 2747.8 jit_solution(8802034476952752222)
XLA Ops:
  11.3 3.7 convolution_convert_fusion.6
  25.3 3.3 fusion.95
  29.7 5.0 reduce-window.6
  36.9 15.5 scatter_custom_fusion
  53.3 63.7 %all-reduce.19.cloned.1.call-done = f32[512,2048]{1,0:T(8,128)} async-done(((f32[512,2048]{1,0:T(8,128)}), f32[512,2048]{1,0:T(8,128)}) %all-reduce.19.cloned.1.call-update) | async-done | bytes 4194320 | tf_op jit(solution)/shard_map/psum | solution.py:119
  117.0 3.5 multiply_reduce_fusion.3
  124.1 36.9 %gather_fusion = bf16[4608,2048]{1,0:T(8,128)(2,1)} fusion(bf16[513,2048]{1,0:T(8,128)(2,1)} %concatenate.39, s32[5120]{0:T(1024)S(1)} %get-tuple-element.104), kind=kCustom, calls=%fused_computation.16 | custom fusion | bytes 37767168 | tf_op jit(solution)/shard_map/jit(_take)/gather | solution.py:131
  161.0 9.7 broadcast_select_fusion
  170.8 413.4 %all_to_all.20 = bf16[8,2,288,2048]{3,2,1,0:T(8,128)(2,1)} all-to-all(bf16[8,2,288,2048]{3,2,1,0:T(8,128)(2,1)S(1)} %broadcast_select_fusion), channel_id=1, replica_groups=mesh['expert'=8,'tensor'=4] {'expert'}, dimensions={0} | all-to-all | bytes 37748736 | tf_op jit(solution)/shard_map/all_to_all | solution.py:134
  584.2 16.5 fusion.42
  600.7 4.5 multiply_convert_fusion.1
  605.2 9.1 convert_bitcast_fusion.1
  614.3 16.9 copy.110
  631.2 5.9 all-to-all-start.1
  637.1 4.1 concatenate.42
  641.3 36.4 %gather_fusion.2 = f32[4608,2048]{1,0:T(8,128)} fusion(f32[513,2048]{1,0:T(8,128)} %concatenate.42, s32[5120]{0:T(1024)S(1)} %get-tuple-element.104), kind=kCustom, calls=%fused_computation.18 | custom fusion | bytes 75515904 | tf_op jit(solution)/shard_map/jit(_take)/gather | solution.py:161
  681.5 362.4 %all-to-all-done.1 = bf16[8,2,288,2048]{3,2,1,0:T(8,128)(2,1)} async-done(((bf16[8,2,288,2048]{3,2,1,0:T(8,128)(2,1)}), bf16[8,2,288,2048]{3,2,1,0:T(8,128)(2,1)}, u32[]{:S(2)}, u32[]{:S(2)}) %all-to-all-start.1) | async-done | bytes 18874400 | tf_op jit(solution)/shard_map/all_to_all | solution.py:147
  1044.0 16.9 concatenate.40
  1060.9 14.0 gather_fusion.10
  1074.9 14.2 gather_fusion.9
  1089.1 14.0 gather_fusion.8
  1103.2 14.4 gather_fusion.7
  1117.6 14.1 gather_fusion.6
  1131.7 14.1 gather_fusion.5
  1145.8 14.2 gather_fusion.4
  1160.0 14.0 gather_fusion.3
  1174.1 8.9 fusion.41
  1183.1 10.1 psum.52
  1194.1 24.1 gather_fusion.1
  1218.4 14.2 multiply_convert_fusion
  1232.6 412.0 %all_to_all.21 = bf16[8,2,288,2048]{3,2,1,0:T(8,128)(2,1)} all-to-all(bf16[8,2,288,2048]{3,2,1,0:T(8,128)(2,1)S(1)} %multiply_convert_fusion), channel_id=1, replica_groups=mesh['expert'=8,'tensor'=4] {'expert'}, dimensions={0} | all-to-all | bytes 37748736 | tf_op jit(solution)/shard_map/all_to_all | solution.py:162
  1644.6 14.0 fusion.12
  1658.6 15.6 convert_bitcast_fusion
  1674.2 9.3 copy.113
  1683.5 411.1 %all_to_all.22 = bf16[8,2,288,2048]{3,2,1,0:T(8,128)(2,1)S(1)} all-to-all(bf16[8,2,288,2048]{3,2,1,0:T(8,128)(2,1)S(1)} %copy.113), channel_id=1, replica_groups=mesh['expert'=8,'tensor'=4] {'expert'}, dimensions={0} | all-to-all | bytes 37748736 | tf_op jit(solution)/shard_map/all_to_all | solution.py:184
  2094.6 8.1 concatenate.44
  2102.7 13.2 gather_fusion.18
  2115.9 14.3 gather_fusion.17
  2130.2 14.0 gather_fusion.16
  2144.2 14.1 gather_fusion.15
  2158.3 14.3 gather_fusion.14
  2172.6 14.1 gather_fusion.13
  2186.7 14.4 gather_fusion.12
  2201.2 14.1 gather_fusion.11
  2215.3 8.4 convert_add_fusion.2
  2226.5 10.0 fusion.29
  2236.6 70.6 %all-reduce.21.cloned.1.call-done = f32[512,2048]{1,0:T(8,128)} async-done(((f32[512,2048]{1,0:T(8,128)}), f32[512,2048]{1,0:T(8,128)}) %all-reduce.21.cloned.1.call-update) | async-done | bytes 4194320 | tf_op jit(solution)/shard_map/psum | solution.py:190
  2307.2 4.9 multiply_reduce_fusion
  2333.0 4.9 convolution_convert_fusion
  2338.0 3.9 convolution_convert_fusion.1
  2343.9 21.3 reduce-scatter.14.cloned.1.call-done
  2369.4 17.9 fusion.17
  2390.2 11.3 fusion.45
  2401.5 51.8 %all-reduce.23.cloned.1.call-done = (bf16[512,2048]{1,0:T(8,128)(2,1)}, bf16[512,2048]{1,0:T(8,128)(2,1)}) async-done(((bf16[512,2048]{1,0:T(8,128)(2,1)}, bf16[512,2048]{1,0:T(8,128)(2,1)}), (bf16[512,2048]{1,0:T(8,128)(2,1)}, bf16[512,2048]{1,0:T(8,128)(2,1)})) %all-reduce.23.cloned.1.call-update) | async-done | bytes 4194320 | tf_op jit(solution)/shard_map/psum | solution.py:155
  2453.3 2.9 fusion.32
  2456.2 22.2 all-reduce.12
  2478.5 7.6 fusion.91
  2486.1 6.0 all-reduce.13
  2494.4 4.4 add_convert_fusion.1
  2500.0 3.3 fusion.21
  2503.3 22.2 reduce-scatter.12.cloned.1.call-done
  2527.3 69.3 %reduce-scatter.10.cloned.1.call-done = bf16[256,512]{1,0:T(8,128)(2,1)} async-done(((bf16[2048,512]{1,0:T(8,128)(2,1)}), bf16[256,512]{1,0:T(8,128)(2,1)}) %reduce-scatter.10.cloned.1.call-update) | async-done | bytes 262160 | tf_op jit(solution)/shard_map/reduce_scatter | solution.py:257
  2598.4 69.4 %reduce-scatter.6.cloned.1.call-done = bf16[256,512]{1,0:T(8,128)(2,1)} async-done(((bf16[2048,512]{1,0:T(8,128)(2,1)}), bf16[256,512]{1,0:T(8,128)(2,1)}) %reduce-scatter.6.cloned.1.call-update) | async-done | bytes 262160 | tf_op jit(solution)/shard_map/reduce_scatter | solution.py:251
  2669.6 69.2 %reduce-scatter.8.cloned.1.call-done = bf16[256,512]{1,0:T(8,128)(2,1)} async-done(((bf16[2048,512]{1,0:T(8,128)(2,1)}), bf16[256,512]{1,0:T(8,128)(2,1)}) %reduce-scatter.8.cloned.1.call-update) | async-done | bytes 262160 | tf_op jit(solution)/shard_map/reduce_scatter | solution.py:254
  (356 shorter events, 68.3 us)
Async XLA Ops:
  7.2 598.0 %copy-start = (bf16[2,256,2048]{2,1,0:T(8,128)(2,1)S(1)}, bf16[2,256,2048]{2,1,0:T(8,128)(2,1)}, u32[]{:S(2)}) copy-start(bf16[2,256,2048]{2,1,0:T(8,128)(2,1)} %param.33) | copy-start | bytes 6291460
  7.2 109.8 %all-reduce.19.cloned.1.call-start = ((), (), s32[]{:S(2)}) async-start(), calls=%async_computation.9 | async-start | bytes 8388608 | tf_op jit(solution)/shard_map/psum | solution.py:119
  9.5 7.6 copy-start.78
  11.3 11.8 copy-start.21
  15.0 8.0 copy-start.45
  52.6 67.9 %copy-start.52 = (s32[8,2,288]{2,1,0:T(2,128)}, s32[8,2,288]{2,1,0:T(2,128)S(1)}, u32[]{:S(2)}) copy-start(s32[8,2,288]{2,1,0:T(2,128)S(1)} %slice.99) | copy-start | bytes 55300
  53.3 107.7 %copy-start.63 = (pred[8,2,288]{2,1,0:T(4,128)(4,1)}, pred[8,2,288]{2,1,0:T(4,128)(4,1)S(1)}, u32[]{:S(2)}) copy-start(pred[8,2,288]{2,1,0:T(4,128)(4,1)S(1)} %compare_and_fusion) | copy-start | bytes 13828
  53.3 67.2 %copy-start.66 = (f32[2048]{0:T(1024)S(1)}, f32[2048]{0:T(1024)}, u32[]{:S(2)}) copy-start(f32[2048]{0:T(1024)} %param.29) | copy-start | bytes 24580
  605.2 9.1 copy-start.19
  631.2 412.7 %all-to-all-start.1 = ((bf16[8,2,288,2048]{3,2,1,0:T(8,128)(2,1)}), bf16[8,2,288,2048]{3,2,1,0:T(8,128)(2,1)}, u32[]{:S(2)}, u32[]{:S(2)}) async-start(bf16[8,2,288,2048]{3,2,1,0:T(8,128)(2,1)} %copy.110), calls=%async_computation.1 | async-start | bytes 37748736 | tf_op jit(solution)/shard_map/all_to_all | solution.py:147
  637.1 1670.1 %all-reduce.21.cloned.1.call-start = ((), (), s32[]{:S(2)}) async-start(), calls=%async_computation.10 | async-start | bytes 8388608 | tf_op jit(solution)/shard_map/psum | solution.py:190
  641.3 36.4 %copy-start.13 = (s32[512,8]{1,0:T(8,128)S(1)}, s32[512,8]{1,0:T(8,128)}, u32[]{:S(2)}) copy-start(s32[512,8]{1,0:T(8,128)} %get-tuple-element.67) | copy-start | bytes 49156
  641.3 37.9 %copy-start.48 = (bf16[2048,16]{0,1:T(8,128)(2,1)S(1)}, bf16[2048,16]{0,1:T(8,128)(2,1)}, u32[]{:S(2)}) copy-start(bf16[2048,16]{0,1:T(8,128)(2,1)} %param.30) | copy-start | bytes 196612
  678.8 467.0 %copy-start.80 = (s32[1024]{0:T(1024)}, s32[1024]{0:T(1024)S(1)}, u32[]{:S(2)}) copy-start(s32[1024]{0:T(1024)S(1)} %pad_clamp_fusion.8) | copy-start | bytes 12292
  678.8 438.8 %copy-start.82 = (s32[1024]{0:T(1024)}, s32[1024]{0:T(1024)S(1)}, u32[]{:S(2)}) copy-start(s32[1024]{0:T(1024)S(1)} %pad_clamp_fusion.6) | copy-start | bytes 12292
  678.9 410.3 %copy-start.86 = (s32[1024]{0:T(1024)}, s32[1024]{0:T(1024)S(1)}, u32[]{:S(2)}) copy-start(s32[1024]{0:T(1024)S(1)} %pad_clamp_fusion.4) | copy-start | bytes 12292
  678.9 382.0 %copy-start.90 = (s32[1024]{0:T(1024)}, s32[1024]{0:T(1024)S(1)}, u32[]{:S(2)}) copy-start(s32[1024]{0:T(1024)S(1)} %pad_clamp_fusion.2) | copy-start | bytes 12292
  678.9 481.1 %copy-start.84 = (s32[1024]{0:T(1024)}, s32[1024]{0:T(1024)S(1)}, u32[]{:S(2)}) copy-start(s32[1024]{0:T(1024)S(1)} %pad_clamp_fusion.9) | copy-start | bytes 12292
  678.9 452.8 %copy-start.88 = (s32[1024]{0:T(1024)}, s32[1024]{0:T(1024)S(1)}, u32[]{:S(2)}) copy-start(s32[1024]{0:T(1024)S(1)} %pad_clamp_fusion.7) | copy-start | bytes 12292
  679.0 424.2 %copy-start.92 = (s32[1024]{0:T(1024)}, s32[1024]{0:T(1024)S(1)}, u32[]{:S(2)}) copy-start(s32[1024]{0:T(1024)S(1)} %pad_clamp_fusion.5) | copy-start | bytes 12292
  679.0 395.9 %copy-start.94 = (s32[1024]{0:T(1024)}, s32[1024]{0:T(1024)S(1)}, u32[]{:S(2)}) copy-start(s32[1024]{0:T(1024)S(1)} %pad_clamp_fusion.3) | copy-start | bytes 12292
  679.0 495.0 %copy-start.96 = (pred[512]{0:T(512)(128)(4,1)}, pred[512]{0:T(512)(128)(4,1)S(1)}, u32[]{:S(2)}) copy-start(pred[512]{0:T(512)(128)(4,1)S(1)} %get-tuple-element.113) | copy-start | bytes 1540
  679.0 495.0 %copy-start.98 = (pred[512]{0:T(512)(128)(4,1)}, pred[512]{0:T(512)(128)(4,1)S(1)}, u32[]{:S(2)}) copy-start(pred[512]{0:T(512)(128)(4,1)S(1)} %get-tuple-element.114) | copy-start | bytes 1540
  679.1 495.0 %copy-start.100 = (pred[512]{0:T(512)(128)(4,1)}, pred[512]{0:T(512)(128)(4,1)S(1)}, u32[]{:S(2)}) copy-start(pred[512]{0:T(512)(128)(4,1)S(1)} %get-tuple-element.115) | copy-start | bytes 1540
  679.1 495.0 %copy-start.102 = (pred[512]{0:T(512)(128)(4,1)}, pred[512]{0:T(512)(128)(4,1)S(1)}, u32[]{:S(2)}) copy-start(pred[512]{0:T(512)(128)(4,1)S(1)} %get-tuple-element.116) | copy-start | bytes 1540
  679.1 495.0 %copy-start.104 = (pred[512]{0:T(512)(128)(4,1)}, pred[512]{0:T(512)(128)(4,1)S(1)}, u32[]{:S(2)}) copy-start(pred[512]{0:T(512)(128)(4,1)S(1)} %get-tuple-element.117) | copy-start | bytes 1540
  679.1 495.0 %copy-start.106 = (pred[512]{0:T(512)(128)(4,1)}, pred[512]{0:T(512)(128)(4,1)S(1)}, u32[]{:S(2)}) copy-start(pred[512]{0:T(512)(128)(4,1)S(1)} %get-tuple-element.118) | copy-start | bytes 1540
  679.1 495.0 %copy-start.108 = (pred[512]{0:T(512)(128)(4,1)}, pred[512]{0:T(512)(128)(4,1)S(1)}, u32[]{:S(2)}) copy-start(pred[512]{0:T(512)(128)(4,1)S(1)} %get-tuple-element.119) | copy-start | bytes 1540
  679.2 495.0 %copy-start.110 = (pred[512]{0:T(512)(128)(4,1)}, pred[512]{0:T(512)(128)(4,1)S(1)}, u32[]{:S(2)}) copy-start(pred[512]{0:T(512)(128)(4,1)S(1)} %get-tuple-element.120) | copy-start | bytes 1540
  1174.1 20.0 copy-start.65
  1193.8 24.4 copy-start.50
  1194.1 24.2 copy-start.53
  1194.1 24.3 copy-start.64
  2094.6 8.1 copy-start.91
  2102.7 13.2 copy-start.95
  2115.9 14.3 copy-start.87
  2130.2 14.0 copy-start.93
  2144.2 14.1 copy-start.83
  2158.3 14.3 copy-start.89
  2172.6 14.1 copy-start.81
  2186.7 14.4 copy-start.85
  2201.1 14.1 copy-start.97
  2201.1 14.1 copy-start.99
  2201.1 14.1 copy-start.101
  2201.1 14.1 copy-start.103
  2201.1 14.1 copy-start.105
  2201.1 14.1 copy-start.107
  2201.2 14.1 copy-start.109
  2201.2 14.1 copy-start.111
  2223.8 141.4 %reduce-scatter.14.cloned.1.call-start = ((), (), s32[]{:S(2)}) async-start(), calls=%async_computation.15 | async-start | bytes 73728 | tf_op jit(solution)/shard_map/reduce_scatter | solution.py:263
  2226.4 226.9 %all-reduce.23.cloned.1.call-start = ((), (), s32[]{:S(2)}) async-start(), calls=%async_computation.16 | async-start | bytes 8388608 | tf_op jit(solution)/shard_map/psum | solution.py:155
  2226.5 80.7 %copy-start.49 = (bf16[2048,16]{0,1:T(8,128)(2,1)S(1)}, bf16[2048,16]{0,1:T(8,128)(2,1)}, u32[]{:S(2)}) copy-start(bf16[2048,16]{0,1:T(8,128)(2,1)} %param.30) | copy-start | bytes 196612
  2226.5 80.7 %copy-start.67 = (f32[2048]{0:T(1024)S(1)}, f32[2048]{0:T(1024)}, u32[]{:S(2)}) copy-start(f32[2048]{0:T(1024)} %param.29) | copy-start | bytes 24580
  2226.5 80.7 %copy-start.77 = (f32[512]{0:T(512)S(1)}, f32[512]{0:T(512)}, u32[]{:S(2)}) copy-start(f32[512]{0:T(512)} %copy-done.76) | copy-start | bytes 6148
  2236.5 75.5 %copy-start.14 = (bf16[512,2048]{1,0:T(8,128)(2,1)S(1)}, bf16[512,2048]{1,0:T(8,128)(2,1)}, u32[]{:S(2)}) copy-start(bf16[512,2048]{1,0:T(8,128)(2,1)} %param.21) | copy-start | bytes 6291460
  2318.7 10.4 copy-start.47
  2332.0 6.0 copy-start.11
  2332.0 193.5 %reduce-scatter.12.cloned.1.call-start = ((), (), s32[]{:S(2)}) async-start(), calls=%async_computation.14 | async-start | bytes 2359296 | tf_op jit(solution)/shard_map/reduce_scatter | solution.py:260
  2337.9 28.6 %copy-start.30 = (bf16[512,4,128]{0,2,1:T(8,128)(2,1)S(1)}, bf16[512,4,128]{0,2,1:T(8,128)(2,1)}, u32[]{:S(2)}) copy-start(bf16[512,4,128]{0,2,1:T(8,128)(2,1)} %copy-done.29) | copy-start | bytes 1572868
  2337.9 258.7 %reduce-scatter.10.cloned.1.call-start = ((), (), s32[]{:S(2)}) async-start(), calls=%async_computation.13 | async-start | bytes 2359296 | tf_op jit(solution)/shard_map/reduce_scatter | solution.py:257
  2342.0 325.8 %reduce-scatter.6.cloned.1.call-start = ((), (), s32[]{:S(2)}) async-start(), calls=%async_computation.11 | async-start | bytes 2359296 | tf_op jit(solution)/shard_map/reduce_scatter | solution.py:251
  2369.4 369.4 %reduce-scatter.8.cloned.1.call-start = ((), (), s32[]{:S(2)}) async-start(), calls=%async_computation.12 | async-start | bytes 2359296 | tf_op jit(solution)/shard_map/reduce_scatter | solution.py:254
  2478.5 15.9 copy-start.42
  2500.0 240.6 %copy-start.1 = (bf16[2,256,2048]{2,1,0:T(8,128)(2,1)S(1)}, bf16[2,256,2048]{2,1,0:T(8,128)(2,1)}, u32[]{:S(2)}) copy-start(bf16[2,256,2048]{2,1,0:T(8,128)(2,1)} %param.33) | copy-start | bytes 6291460
  (63 other events, 141.9 us)
Sparse Core Ops, SparseCore 0:
  28.8 88.1 all-reduce.18
  2223.9 83.1 all-reduce.20
  2310.3 54.8 reduce-scatter.13
  2368.7 84.5 all-reduce.22
  2456.7 68.7 reduce-scatter.11
  2528.9 67.6 reduce-scatter.9
  2600.1 67.6 reduce-scatter.5
  2671.3 67.3 reduce-scatter.7
where the time goes:
time: 2760 us; the launch traced here: 2750 us
  blocking collectives  1270 us (46%)
  waiting for transfers between devices  800 us (29%)
  local copies, waits for them, and re-layouts  420 us (15%)
  matrix products  130 us (5%)
  other arithmetic  99.7 us (4%)
    all_to_all x1, blocking collectives, on_device(): lax.all_to_all(send_buf, 'expert', split_axis=0, concat_axis=0, tiled=True)  413 us
    all_to_all x1, blocking collectives, on_device(): lax.all_to_all(grad_buf.reshape(expert_ranks, local_experts, capacity, mo...  412 us
    all_to_all x1, blocking collectives, on_device(): lax.all_to_all(dslot_in, 'expert', split_axis=0, concat_axis=0, tiled=True)  411 us
    all_to_all x1, waiting for transfers between devices, on_device(): lax.all_to_all(partial_out, 'expert', split_axis=0, concat_axis=0, tiled=...  362 us
    gather x8, local copies, waits for them, and re-layouts, on_device(): picked = jnp.take(returned, slot_ids[:, rank_k], axis=0)  113 us
    gather x8, local copies, waits for them, and re-layouts, on_device(): jnp.take(came_back, slot_ids[:, rank_k], axis=0)  112 us
    psum x1, waiting for transfers between devices, on_device(): dnormed_exp, dgate_all = lax.psum((dnormed_part, dgate_part), 'tensor')  70.6 us
    reduce_scatter x1, waiting for transfers between devices, on_device(): lax.psum_scatter(q_grad.astype(jnp.bfloat16), 'expert', scatter_dimension...  69.4 us
  transfers between devices with their start and end apart: 9, of which 9 were waited for; matrix products, arithmetic and copies ran while one was open for 6% of the time, Pallas kernels for 0%

commit v1 on v0

--- a/solution.py
+++ b/solution.py
@@ -116,7 +116,11 @@
     attn_part = lax.dot_general(
         attn_out, o_weight, (((1,), (1,)), ((), ())), preferred_element_type=jnp.float32
     )
-    attn_full = lax.psum(attn_part, "tensor")
+    attn_full = attn_part
+    for hop in (1, 2):
+        attn_full = attn_full + lax.ppermute(
+            attn_full, "tensor", [(dev, dev ^ hop) for dev in range(4)]
+        )
     after_attn = inputs + attn_full
     scale_two = rms_scale(after_attn)
     unit_two = after_attn * scale_two

time: 2760 us -> 2660 us (0.964)
  waiting for transfers between devices: 800 us -> 691 us
    ppermute x0 -> x2, waiting for transfers between devices: none -> 74 us  [on_device(): lax.ppermute(attn_full, 'tensor', [(dev, dev ^ hop) for dev in range(4)])]
    psum x1 -> x0, waiting for transfers between devices: 63.7 us -> none  [on_device(): attn_full = lax.psum(attn_part, 'tensor')]
    reduce_scatter x1, waiting for transfers between devices: 69.3 us -> 7.89 us  [on_device(): lax.psum_scatter(v_grad.astype(jnp.bfloat16), 'expert', scatter_dimension...]
  transfers between devices with their start and end apart: 9 -> 10, of which waited for: 9 -> 8; matrix products, arithmetic and copies ran while one was open for 6% -> 6% of each run, Pallas kernels for 0% -> 0%
where the time goes in v1:
time: 2660 us; the launch traced here: 2650 us
  blocking collectives  1280 us (48%)
  waiting for transfers between devices  691 us (26%)
  local copies, waits for them, and re-layouts  419 us (16%)
  matrix products  128 us (5%)
  other arithmetic  104 us (4%)
    all_to_all x1, blocking collectives, on_device(): lax.all_to_all(send_buf, 'expert', split_axis=0, concat_axis=0, tiled=True)  414 us
    all_to_all x1, blocking collectives, on_device(): lax.all_to_all(grad_buf.reshape(expert_ranks, local_experts, capacity, mo...  412 us
    all_to_all x1, blocking collectives, on_device(): lax.all_to_all(dslot_in, 'expert', split_axis=0, concat_axis=0, tiled=True)  411 us
    all_to_all x1, waiting for transfers between devices, on_device(): lax.all_to_all(partial_out, 'expert', split_axis=0, concat_axis=0, tiled=...  362 us
    gather x8, local copies, waits for them, and re-layouts, on_device(): picked = jnp.take(returned, slot_ids[:, rank_k], axis=0)  113 us
    gather x8, local copies, waits for them, and re-layouts, on_device(): jnp.take(came_back, slot_ids[:, rank_k], axis=0)  112 us
    ppermute x2, waiting for transfers between devices, on_device(): lax.ppermute(attn_full, 'tensor', [(dev, dev ^ hop) for dev in range(4)])  74 us
    psum x1, waiting for transfers between devices, on_device(): dnormed_exp, dgate_all = lax.psum((dnormed_part, dgate_part), 'tensor')  70.6 us
  transfers between devices with their start and end apart: 10, of which 8 were waited for; matrix products, arithmetic and copies ran while one was open for 6% of the time, Pallas kernels for 0%

profile of v1, /device:TPU:0, one launch (start us, length us, event | category | flops | bytes accessed | tf_op | source)
XLA Modules:
  0.0 2645.7 jit_solution(11649631374275442538)
XLA Ops:
  12.1 3.7 convolution_convert_fusion.6
  28.0 6.8 collective-permute-done
  37.6 2.9 collective-permute-start.1
  40.9 5.0 reduce-window.6
  48.0 15.5 scatter_custom_fusion
  64.4 67.2 %collective-permute-done.1 = f32[512,2048]{1,0:T(8,128)} collective-permute-done((f32[512,2048]{1,0:T(8,128)}, f32[512,2048]{1,0:T(8,128)}, u32[]{:S(2)}, u32[]{:S(2)}) %collective-permute-start.1) | collective-permute-done | bytes 4194336 | tf_op jit(solution)/shard_map/ppermute | solution.py:121
  131.6 4.8 multiply_reduce_fusion.3
  140.0 36.9 %gather_fusion = bf16[4608,2048]{1,0:T(8,128)(2,1)} fusion(bf16[513,2048]{1,0:T(8,128)(2,1)} %concatenate.39, s32[5120]{0:T(1024)S(1)} %get-tuple-element.104), kind=kCustom, calls=%fused_computation.16 | custom fusion | bytes 37767168 | tf_op jit(solution)/shard_map/jit(_take)/gather | solution.py:135
  176.9 9.7 broadcast_select_fusion
  186.7 413.8 %all_to_all.20 = bf16[8,2,288,2048]{3,2,1,0:T(8,128)(2,1)} all-to-all(bf16[8,2,288,2048]{3,2,1,0:T(8,128)(2,1)S(1)} %broadcast_select_fusion), channel_id=1, replica_groups=mesh['expert'=8,'tensor'=4] {'expert'}, dimensions={0} | all-to-all | bytes 37748736 | tf_op jit(solution)/shard_map/all_to_all | solution.py:138
  600.5 16.6 fusion.42
  617.0 4.5 multiply_convert_fusion.1
  621.5 9.1 convert_bitcast_fusion.1
  630.6 17.0 copy.110
  647.6 5.9 all-to-all-start.1
  653.5 4.1 concatenate.42
  657.7 36.4 %gather_fusion.2 = f32[4608,2048]{1,0:T(8,128)} fusion(f32[513,2048]{1,0:T(8,128)} %concatenate.42, s32[5120]{0:T(1024)S(1)} %get-tuple-element.104), kind=kCustom, calls=%fused_computation.18 | custom fusion | bytes 75515904 | tf_op jit(solution)/shard_map/jit(_take)/gather | solution.py:165
  697.9 362.3 %all-to-all-done.1 = bf16[8,2,288,2048]{3,2,1,0:T(8,128)(2,1)} async-done(((bf16[8,2,288,2048]{3,2,1,0:T(8,128)(2,1)}), bf16[8,2,288,2048]{3,2,1,0:T(8,128)(2,1)}, u32[]{:S(2)}, u32[]{:S(2)}) %all-to-all-start.1) | async-done | bytes 18874400 | tf_op jit(solution)/shard_map/all_to_all | solution.py:151
  1060.2 16.9 concatenate.40
  1077.2 14.0 gather_fusion.10
  1091.2 14.2 gather_fusion.9
  1105.4 14.0 gather_fusion.8
  1119.5 14.4 gather_fusion.7
  1133.9 14.1 gather_fusion.6
  1148.0 14.1 gather_fusion.5
  1162.1 14.2 gather_fusion.4
  1176.3 14.0 gather_fusion.3
  1190.4 8.9 fusion.41
  1199.4 10.1 psum.44
  1210.4 24.1 gather_fusion.1
  1234.7 14.2 multiply_convert_fusion
  1248.9 412.4 %all_to_all.21 = bf16[8,2,288,2048]{3,2,1,0:T(8,128)(2,1)} all-to-all(bf16[8,2,288,2048]{3,2,1,0:T(8,128)(2,1)S(1)} %multiply_convert_fusion), channel_id=1, replica_groups=mesh['expert'=8,'tensor'=4] {'expert'}, dimensions={0} | all-to-all | bytes 37748736 | tf_op jit(solution)/shard_map/all_to_all | solution.py:166
  1661.2 13.9 fusion.12
  1675.2 15.6 convert_bitcast_fusion
  1690.8 9.3 copy.113
  1700.1 411.1 %all_to_all.22 = bf16[8,2,288,2048]{3,2,1,0:T(8,128)(2,1)S(1)} all-to-all(bf16[8,2,288,2048]{3,2,1,0:T(8,128)(2,1)S(1)} %copy.113), channel_id=1, replica_groups=mesh['expert'=8,'tensor'=4] {'expert'}, dimensions={0} | all-to-all | bytes 37748736 | tf_op jit(solution)/shard_map/all_to_all | solution.py:188
  2111.2 8.1 concatenate.44
  2119.3 13.2 gather_fusion.18
  2132.6 14.2 gather_fusion.17
  2146.8 14.0 gather_fusion.16
  2160.9 14.1 gather_fusion.15
  2175.0 14.3 gather_fusion.14
  2189.3 14.1 gather_fusion.13
  2203.3 14.4 gather_fusion.12
  2217.9 14.1 gather_fusion.11
  2232.0 8.4 convert_add_fusion.2
  2243.2 10.1 fusion.29
  2253.3 70.6 %all-reduce.18.cloned.1.call-done = f32[512,2048]{1,0:T(8,128)} async-done(((f32[512,2048]{1,0:T(8,128)}), f32[512,2048]{1,0:T(8,128)}) %all-reduce.18.cloned.1.call-update) | async-done | bytes 4194320 | tf_op jit(solution)/shard_map/psum | solution.py:194
  2323.9 4.9 multiply_reduce_fusion
  2349.8 4.8 convolution_convert_fusion
  2354.7 4.0 convolution_convert_fusion.1
  2365.0 17.4 fusion.17
  2382.3 2.9 convolution_convert_fusion.2
  2385.2 11.5 fusion.45
  2396.7 37.9 %all-reduce.20.cloned.1.call-done = (bf16[512,2048]{1,0:T(8,128)(2,1)}, bf16[512,2048]{1,0:T(8,128)(2,1)}) async-done(((bf16[512,2048]{1,0:T(8,128)(2,1)}, bf16[512,2048]{1,0:T(8,128)(2,1)}), (bf16[512,2048]{1,0:T(8,128)(2,1)}, bf16[512,2048]{1,0:T(8,128)(2,1)})) %all-reduce.20.cloned.1.call-update) | async-done | bytes 4194320 | tf_op jit(solution)/shard_map/psum | solution.py:159
  2434.6 2.9 fusion.32
  2437.5 22.5 all-reduce.12
  2460.2 7.5 fusion.91
  2467.7 5.8 all-reduce.13
  2475.8 4.4 add_convert_fusion.1
  2481.4 3.3 fusion.21
  2486.5 7.9 reduce-scatter.10.cloned.1.call-done
  2496.1 69.2 %reduce-scatter.6.cloned.1.call-done = bf16[256,512]{1,0:T(8,128)(2,1)} async-done(((bf16[2048,512]{1,0:T(8,128)(2,1)}), bf16[256,512]{1,0:T(8,128)(2,1)}) %reduce-scatter.6.cloned.1.call-update) | async-done | bytes 262160 | tf_op jit(solution)/shard_map/reduce_scatter | solution.py:255
  2567.1 68.9 %reduce-scatter.8.cloned.1.call-done = bf16[256,512]{1,0:T(8,128)(2,1)} async-done(((bf16[2048,512]{1,0:T(8,128)(2,1)}), bf16[256,512]{1,0:T(8,128)(2,1)}) %reduce-scatter.8.cloned.1.call-update) | async-done | bytes 262160 | tf_op jit(solution)/shard_map/reduce_scatter | solution.py:258
  (358 shorter events, 69.4 us)
Async XLA Ops:
  8.0 613.5 %copy-start = (bf16[2,256,2048]{2,1,0:T(8,128)(2,1)S(1)}, bf16[2,256,2048]{2,1,0:T(8,128)(2,1)}, u32[]{:S(2)}) copy-start(bf16[2,256,2048]{2,1,0:T(8,128)(2,1)} %param.33) | copy-start | bytes 6291460
  10.3 7.6 copy-start.78
  12.1 11.7 copy-start.21
  15.8 8.0 copy-start.45
  27.4 13.0 copy-start.56
  27.4 7.3 collective-permute-start
  37.6 94.1 %collective-permute-start.1 = (f32[512,2048]{1,0:T(8,128)}, f32[512,2048]{1,0:T(8,128)}, u32[]{:S(2)}, u32[]{:S(2)}) collective-permute-start(f32[512,2048]{1,0:T(8,128)} %add.243), channel_id=1, source_target_pairs={{0,2},{1,3},{2,0},{3,1},{4,6},{5,7},{6,4},{7,5},{8,10},{9,11},{10,... | collective-permute-start | bytes 12582920 | tf_op jit(solution)/shard_map/ppermute | solution.py:121
  63.7 72.8 %copy-start.52 = (s32[8,2,288]{2,1,0:T(2,128)}, s32[8,2,288]{2,1,0:T(2,128)S(1)}, u32[]{:S(2)}) copy-start(s32[8,2,288]{2,1,0:T(2,128)S(1)} %slice.99) | copy-start | bytes 55300
  64.4 112.5 %copy-start.63 = (pred[8,2,288]{2,1,0:T(4,128)(4,1)}, pred[8,2,288]{2,1,0:T(4,128)(4,1)S(1)}, u32[]{:S(2)}) copy-start(pred[8,2,288]{2,1,0:T(4,128)(4,1)S(1)} %compare_and_fusion) | copy-start | bytes 13828
  64.4 72.1 %copy-start.66 = (f32[2048]{0:T(1024)S(1)}, f32[2048]{0:T(1024)}, u32[]{:S(2)}) copy-start(f32[2048]{0:T(1024)} %param.29) | copy-start | bytes 24580
  621.5 9.1 copy-start.19
  647.6 412.7 %all-to-all-start.1 = ((bf16[8,2,288,2048]{3,2,1,0:T(8,128)(2,1)}), bf16[8,2,288,2048]{3,2,1,0:T(8,128)(2,1)}, u32[]{:S(2)}, u32[]{:S(2)}) async-start(bf16[8,2,288,2048]{3,2,1,0:T(8,128)(2,1)} %copy.110), calls=%async_computation.1 | async-start | bytes 37748736 | tf_op jit(solution)/shard_map/all_to_all | solution.py:151
  653.5 1670.4 %all-reduce.18.cloned.1.call-start = ((), (), s32[]{:S(2)}) async-start(), calls=%async_computation.9 | async-start | bytes 8388608 | tf_op jit(solution)/shard_map/psum | solution.py:194
  657.7 36.4 %copy-start.13 = (s32[512,8]{1,0:T(8,128)S(1)}, s32[512,8]{1,0:T(8,128)}, u32[]{:S(2)}) copy-start(s32[512,8]{1,0:T(8,128)} %get-tuple-element.67) | copy-start | bytes 49156
  657.7 37.9 %copy-start.48 = (bf16[2048,16]{0,1:T(8,128)(2,1)S(1)}, bf16[2048,16]{0,1:T(8,128)(2,1)}, u32[]{:S(2)}) copy-start(bf16[2048,16]{0,1:T(8,128)(2,1)} %param.30) | copy-start | bytes 196612
  695.2 466.9 %copy-start.80 = (s32[1024]{0:T(1024)}, s32[1024]{0:T(1024)S(1)}, u32[]{:S(2)}) copy-start(s32[1024]{0:T(1024)S(1)} %pad_clamp_fusion.8) | copy-start | bytes 12292
  695.2 438.7 %copy-start.82 = (s32[1024]{0:T(1024)}, s32[1024]{0:T(1024)S(1)}, u32[]{:S(2)}) copy-start(s32[1024]{0:T(1024)S(1)} %pad_clamp_fusion.6) | copy-start | bytes 12292
  695.3 410.2 %copy-start.86 = (s32[1024]{0:T(1024)}, s32[1024]{0:T(1024)S(1)}, u32[]{:S(2)}) copy-start(s32[1024]{0:T(1024)S(1)} %pad_clamp_fusion.4) | copy-start | bytes 12292
  695.3 381.9 %copy-start.90 = (s32[1024]{0:T(1024)}, s32[1024]{0:T(1024)S(1)}, u32[]{:S(2)}) copy-start(s32[1024]{0:T(1024)S(1)} %pad_clamp_fusion.2) | copy-start | bytes 12292
  695.3 481.0 %copy-start.84 = (s32[1024]{0:T(1024)}, s32[1024]{0:T(1024)S(1)}, u32[]{:S(2)}) copy-start(s32[1024]{0:T(1024)S(1)} %pad_clamp_fusion.9) | copy-start | bytes 12292
  695.3 452.7 %copy-start.88 = (s32[1024]{0:T(1024)}, s32[1024]{0:T(1024)S(1)}, u32[]{:S(2)}) copy-start(s32[1024]{0:T(1024)S(1)} %pad_clamp_fusion.7) | copy-start | bytes 12292
  695.4 424.1 %copy-start.92 = (s32[1024]{0:T(1024)}, s32[1024]{0:T(1024)S(1)}, u32[]{:S(2)}) copy-start(s32[1024]{0:T(1024)S(1)} %pad_clamp_fusion.5) | copy-start | bytes 12292
  695.4 395.8 %copy-start.94 = (s32[1024]{0:T(1024)}, s32[1024]{0:T(1024)S(1)}, u32[]{:S(2)}) copy-start(s32[1024]{0:T(1024)S(1)} %pad_clamp_fusion.3) | copy-start | bytes 12292
  695.4 495.0 %copy-start.96 = (pred[512]{0:T(512)(128)(4,1)}, pred[512]{0:T(512)(128)(4,1)S(1)}, u32[]{:S(2)}) copy-start(pred[512]{0:T(512)(128)(4,1)S(1)} %get-tuple-element.113) | copy-start | bytes 1540
  695.4 495.0 %copy-start.98 = (pred[512]{0:T(512)(128)(4,1)}, pred[512]{0:T(512)(128)(4,1)S(1)}, u32[]{:S(2)}) copy-start(pred[512]{0:T(512)(128)(4,1)S(1)} %get-tuple-element.114) | copy-start | bytes 1540
  695.5 494.9 %copy-start.100 = (pred[512]{0:T(512)(128)(4,1)}, pred[512]{0:T(512)(128)(4,1)S(1)}, u32[]{:S(2)}) copy-start(pred[512]{0:T(512)(128)(4,1)S(1)} %get-tuple-element.115) | copy-start | bytes 1540
  695.5 494.9 %copy-start.102 = (pred[512]{0:T(512)(128)(4,1)}, pred[512]{0:T(512)(128)(4,1)S(1)}, u32[]{:S(2)}) copy-start(pred[512]{0:T(512)(128)(4,1)S(1)} %get-tuple-element.116) | copy-start | bytes 1540
  695.5 494.9 %copy-start.104 = (pred[512]{0:T(512)(128)(4,1)}, pred[512]{0:T(512)(128)(4,1)S(1)}, u32[]{:S(2)}) copy-start(pred[512]{0:T(512)(128)(4,1)S(1)} %get-tuple-element.117) | copy-start | bytes 1540
  695.5 494.9 %copy-start.106 = (pred[512]{0:T(512)(128)(4,1)}, pred[512]{0:T(512)(128)(4,1)S(1)}, u32[]{:S(2)}) copy-start(pred[512]{0:T(512)(128)(4,1)S(1)} %get-tuple-element.118) | copy-start | bytes 1540
  695.5 494.9 %copy-start.108 = (pred[512]{0:T(512)(128)(4,1)}, pred[512]{0:T(512)(128)(4,1)S(1)}, u32[]{:S(2)}) copy-start(pred[512]{0:T(512)(128)(4,1)S(1)} %get-tuple-element.119) | copy-start | bytes 1540
  695.6 494.9 %copy-start.110 = (pred[512]{0:T(512)(128)(4,1)}, pred[512]{0:T(512)(128)(4,1)S(1)}, u32[]{:S(2)}) copy-start(pred[512]{0:T(512)(128)(4,1)S(1)} %get-tuple-element.120) | copy-start | bytes 1540
  1190.4 20.0 copy-start.65
  1210.1 24.4 copy-start.50
  1210.4 24.2 copy-start.53
  1210.4 24.3 copy-start.64
  2111.2 8.1 copy-start.91
  2119.3 13.2 copy-start.95
  2132.6 14.3 copy-start.87
  2146.8 14.1 copy-start.93
  2160.9 14.1 copy-start.83
  2175.0 14.3 copy-start.89
  2189.2 14.1 copy-start.81
  2203.3 14.4 copy-start.85
  2217.8 14.1 copy-start.97
  2217.8 14.1 copy-start.99
  2217.8 14.1 copy-start.101
  2217.8 14.1 copy-start.103
  2217.8 14.1 copy-start.105
  2217.8 14.1 copy-start.107
  2217.8 14.1 copy-start.109
  2217.9 14.1 copy-start.111
  2240.5 120.3 %reduce-scatter.14.cloned.1.call-start = ((), (), s32[]{:S(2)}) async-start(), calls=%async_computation.14 | async-start | bytes 73728 | tf_op jit(solution)/shard_map/reduce_scatter | solution.py:267
  2243.1 191.4 %all-reduce.20.cloned.1.call-start = ((), (), s32[]{:S(2)}) async-start(), calls=%async_computation.15 | async-start | bytes 8388608 | tf_op jit(solution)/shard_map/psum | solution.py:159
  2243.2 80.8 %copy-start.49 = (bf16[2048,16]{0,1:T(8,128)(2,1)S(1)}, bf16[2048,16]{0,1:T(8,128)(2,1)}, u32[]{:S(2)}) copy-start(bf16[2048,16]{0,1:T(8,128)(2,1)} %param.30) | copy-start | bytes 196612
  2243.2 80.7 %copy-start.67 = (f32[2048]{0:T(1024)S(1)}, f32[2048]{0:T(1024)}, u32[]{:S(2)}) copy-start(f32[2048]{0:T(1024)} %param.29) | copy-start | bytes 24580
  2243.2 80.7 %copy-start.77 = (f32[512]{0:T(512)S(1)}, f32[512]{0:T(512)}, u32[]{:S(2)}) copy-start(f32[512]{0:T(512)} %copy-done.76) | copy-start | bytes 6148
  2253.3 75.5 %copy-start.14 = (bf16[512,2048]{1,0:T(8,128)(2,1)S(1)}, bf16[512,2048]{1,0:T(8,128)(2,1)}, u32[]{:S(2)}) copy-start(bf16[512,2048]{1,0:T(8,128)(2,1)} %param.21) | copy-start | bytes 6291460
  2335.4 10.4 copy-start.47
  2348.8 135.9 %reduce-scatter.12.cloned.1.call-start = ((), (), s32[]{:S(2)}) async-start(), calls=%async_computation.13 | async-start | bytes 2359296 | tf_op jit(solution)/shard_map/reduce_scatter | solution.py:264
  2354.6 139.7 %reduce-scatter.10.cloned.1.call-start = ((), (), s32[]{:S(2)}) async-start(), calls=%async_computation.12 | async-start | bytes 2359296 | tf_op jit(solution)/shard_map/reduce_scatter | solution.py:261
  2358.8 206.5 %reduce-scatter.6.cloned.1.call-start = ((), (), s32[]{:S(2)}) async-start(), calls=%async_computation.10 | async-start | bytes 2359296 | tf_op jit(solution)/shard_map/reduce_scatter | solution.py:255
  2364.9 271.1 %reduce-scatter.8.cloned.1.call-start = ((), (), s32[]{:S(2)}) async-start(), calls=%async_computation.11 | async-start | bytes 2359296 | tf_op jit(solution)/shard_map/reduce_scatter | solution.py:258
  2460.2 15.6 copy-start.42
  2481.4 156.4 %copy-start.1 = (bf16[2,256,2048]{2,1,0:T(8,128)(2,1)S(1)}, bf16[2,256,2048]{2,1,0:T(8,128)(2,1)}, u32[]{:S(2)}) copy-start(bf16[2,256,2048]{2,1,0:T(8,128)(2,1)} %param.33) | copy-start | bytes 6291460
  (64 other events, 158.1 us)
Sparse Core Ops, SparseCore 0:
  2240.6 83.2 all-reduce.17
  2348.9 85.6 all-reduce.19
Sparse Core Ops, SparseCore 1:
  2244.1 52.6 reduce-scatter.13
  2354.7 68.4 reduce-scatter.11
  2426.6 67.7 reduce-scatter.9
  2497.9 67.4 reduce-scatter.5
  2568.9 67.0 reduce-scatter.7
